TPU v7x, 32 devices: a whole 2x2x4 slice. The times are simulated.
32 devices in a mesh: row: 4 (over x, core), col: 8 (over z, y).
Axes of the slice: x: 2, y: 2, z: 4, core: 2. Of those that a mesh axis runs over, the one named last changes fastest.
Arguments:
- signatures: bfloat16 [2048, 49152], P('row', 'col'), as said below
- trailing: float32 [2048, 1024], P('row', 'col'), may hold values from -6 to 6
- ridge: float32 [1], replicated, may hold values from 0.5 to 2
- panel_index: int32 [1], replicated, may hold values from 1 to 3
Outputs:
- factor: float32 [2048, 256], P(('row', 'col'))
- updated: float32 [2048, 1024], P('row', 'col')
Inputs may be any that keep to these rules, and one draw needn't show every extreme that they name: `signatures`: every diagonal block of the Gram matrix plus the ridge is positive definite.
All inputs are finite; a program needn't handle non-finite values.
Results may differ from a plain program's by a relative error of at most 0.0003.
Values may be sent and summed in bfloat16 or wider, within the bound.
A program may use at most 64 MiB of HBM per device.

v0:
```python
import jax
import jax.numpy as jnp
from jax import lax
from jax.sharding import PartitionSpec as P

PANEL = 256


def spread(block, axis, owner):
    block = jnp.where(lax.axis_index(axis) == owner, block, jnp.zeros_like(block))
    return lax.psum(block, axis)


def add_ridge(block, first_row, panel_start, ridge):
    row_ids = first_row + lax.broadcasted_iota(jnp.int32, block.shape, 0)
    col_ids = panel_start + lax.broadcasted_iota(jnp.int32, block.shape, 1)
    return block + jnp.where(row_ids == col_ids, ridge[0], jnp.zeros((), block.dtype))


def mask_above(block, first_row, panel_start):
    row_ids = first_row + lax.broadcasted_iota(jnp.int32, block.shape, 0)
    return jnp.where(row_ids >= panel_start, block, jnp.zeros((), block.dtype))


def solve_rows(lower, panel_rows):
    return jax.scipy.linalg.solve_triangular(lower, panel_rows.T, lower=True).T


def local(signatures, trailing, ridge, panel_index):
    rows_dev = signatures.shape[0]
    tile_cols = trailing.shape[1]
    col_count = lax.axis_size("col")
    row_share = rows_dev // col_count
    row_pos = lax.axis_index("row")
    col_pos = lax.axis_index("col")
    panel_start = panel_index[0] * PANEL
    row_owner = panel_start // rows_dev
    local_offset = panel_start % rows_dev
    own_paths = lax.dynamic_slice_in_dim(signatures, local_offset, PANEL, 0)
    panel_paths = spread(own_paths, "row", row_owner)
    mine_rows = lax.psum_scatter(
        lax.dot_general(
            signatures, panel_paths, (((1,), (1,)), ((), ())), preferred_element_type=jnp.float32
        ),
        "col",
        scatter_dimension=0,
        tiled=True,
    )
    mine_rows = add_ridge(mine_rows, row_pos * rows_dev + col_pos * row_share, panel_start, ridge)
    own_block = lax.dot_general(
        panel_paths, panel_paths, (((1,), (1,)), ((), ())), preferred_element_type=jnp.float32
    )
    diagonal = lax.psum(own_block, "col")
    diagonal = add_ridge(diagonal, panel_start, panel_start, ridge)
    lower = jnp.linalg.cholesky(diagonal)
    factor_mine = solve_rows(lower, mine_rows)
    factor_mine = mask_above(factor_mine, row_pos * rows_dev + col_pos * row_share, panel_start)
    factor_block = lax.all_gather(factor_mine, "col", axis=0, tiled=True)
    window_start = panel_start + PANEL + col_pos * tile_cols
    window_owner = window_start // rows_dev
    window_cut = lax.dynamic_slice_in_dim(factor_block, window_start % rows_dev, tile_cols, 0)
    window_rows = spread(window_cut, "row", window_owner)
    updated = trailing - lax.dot_general(
        factor_block,
        window_rows,
        (((1,), (1,)), ((), ())),
        precision=lax.Precision.HIGHEST,
        preferred_element_type=jnp.float32,
    )
    return (factor_mine, updated)


def solution(mesh):
    placed = (P("row", "col"), P("row", "col"), P(), P())
    return jax.shard_map(
        local,
        mesh=mesh,
        in_specs=placed,
        out_specs=(P(("row", "col"), None), P("row", "col")),
        check_vma=False,
    )
```

profile of v0, /device:TPU:0, one launch (start us, length us, event | category | flops | bytes accessed | tf_op | source)
XLA Modules:
  0.0 299.6 jit_solution(7277814875881397498)
XLA Ops:
  7.9 4.5 %dynamic-slice_select_fusion = bf16[256,6144]{1,0:T(8,128)(2,1)} fusion(bf16[512,6144]{1,0:T(8,128)(2,1)} %param.4, s32[]{:T(128)S(6)} %select_n.62, pred[]{:T(512)S(6)} %eq.15), kind=kLoop, calls=%fused_computation.2 | loop fusion | flops 1572864 | bytes 6291461 | tf_op jit(solution)/shard_map/jit(_where)/select_n | solution.py:10
  13.3 70.5 %all-reduce.5.cloned.1.call-done = bf16[256,6144]{1,0:T(8,128)(2,1)} async-done(((bf16[256,6144]{1,0:T(8,128)(2,1)}), bf16[256,6144]{1,0:T(8,128)(2,1)}) %all-reduce.5.cloned.1.call-update) | async-done | bytes 3145744 | tf_op jit(solution)/shard_map/psum | solution.py:11
  83.8 4.6 %fusion.10 = f32[256,256]{0,1:T(8,128)} fusion(bf16[256,6144]{1,0:T(8,128)(2,1)} %all-reduce.5.cloned.1.call-done), kind=kOutput, calls=%fused_computation.39 | convolution fusion | flops 805306368 | bytes 3407872 | tf_op jit(solution)/shard_map/dot_general | solution.py:50
  88.4 5.6 %convolution_bitcast_fusion = f32[512,256]{0,1:T(8,128)S(1)} fusion(bf16[256,6144]{1,0:T(8,128)(2,1)} %all-reduce.5.cloned.1.call-done, bf16[512,6144]{1,0:T(8,128)(2,1)} %param.4), kind=kOutput, calls=%fused_computation.3 | convolution fusion | flops 1610612736 | bytes 9961472 | tf_op jit(solution)/shard_map/dot_general | solution.py:42
  94.0 1.0 copy.19
  95.2 64.4 %all-reduce.7.cloned.1.call-done = f32[256,256]{0,1:T(8,128)} async-done(((f32[256,256]{0,1:T(8,128)}), f32[256,256]{0,1:T(8,128)}) %all-reduce.7.cloned.1.call-update) | async-done | bytes 262160 | tf_op jit(solution)/shard_map/psum | solution.py:53
  159.6 1.0 select_add_fusion
  160.8 1.1 fusion
  161.9 11.7 %cholesky.49 = f32[128,128]{1,0:T(8,128)S(1)} custom-call(f32[128,128]{1,0:T(8,128)S(1)} %cholesky.115), custom_call_target="Cholesky" | custom-call | tf_op jit(solution)/shard_map/jit(cholesky)/cholesky | solution.py:55
  173.7 9.8 %custom-call.15 = f32[1,128,128]{1,2,0:T(8,128)S(1)} custom-call(f32[1,128,128]{2,1,0:T(8,128)S(1)} %get-tuple-element.29), custom_call_target="InvertDiagBlocksLowerTriangular" | custom-call | tf_op jit(solution)/shard_map/jit(cholesky)/cholesky | solution.py:55
  184.0 11.7 %cholesky.103 = f32[128,128]{1,0:T(8,128)S(1)} custom-call(f32[128,128]{1,0:T(8,128)S(1)} %convolution_subtract_fusion.2), custom_call_target="Cholesky" | custom-call | tf_op jit(solution)/shard_map/jit(cholesky)/cholesky | solution.py:55
  196.0 0.6 compare_reduce_fusion
  198.1 4.4 %while.1 = (s32[]{:T(128)}, f32[256,256]{0,1:T(8,128)S(1)}, s32[2,2]{1,0:T(2,128)S(1)}, f32[2,128,128]{2,1,0:T(8,128)S(1)}, s32[]{:T(128)}) while((s32[]{:T(128)}, f32[256,256]{0,1:T(8,128)S(1)}, s32[2,2]{1,0:T(2,128)S(1)}, f32[2,128,128]{2,1,0:T(8,128)S(1)}, s32[]{:T(128)}) %tuple.27), condition=%wide.while_cond, body=%wide.while_body.sunk | while | flops 2 | bytes 393321 | solution.py:26
  198.3 0.6 fusion.22
  198.9 1.4 dynamic-slice.7
  200.4 0.6 fusion.22
  201.0 1.4 dynamic-slice.7
  202.5 19.7 %custom-call.16 = f32[2,128,128]{1,2,0:T(8,128)S(1)} custom-call(f32[2,128,128]{2,1,0:T(8,128)S(1)} %get-tuple-element.9), custom_call_target="InvertDiagBlocksLowerTriangular" | custom-call | tf_op jit(solution)/shard_map/jit(_solve_triangular)/triangular_solve | solution.py:26
  222.2 3.6 %reduce-scatter.4.cloned.1.call-done = f32[64,256]{1,0:T(8,128)} async-done(((f32[512,256]{1,0:T(8,128)}), f32[64,256]{1,0:T(8,128)}) %reduce-scatter.4.cloned.1.call-update) | async-done | bytes 65552
  225.8 0.9 copy.20
  227.8 31.4 %all_gather.3 = f32[512,256]{1,0:T(8,128)S(1)} all-gather(f32[64,256]{1,0:T(8,128)S(1)} %fusion.7), channel_id=1, replica_groups=mesh['row'=4,'col'=8] {'col'}, dimensions={0}, use_global_device_ids=true | all-gather | bytes 589824 | tf_op jit(solution)/shard_map/all_gather | solution.py:58
  259.2 0.7 dynamic-slice_select_fusion.1
  259.9 30.9 %all-reduce.9.cloned.1.call-done = f32[128,256]{1,0:T(8,128)} async-done(((f32[128,256]{1,0:T(8,128)}), f32[128,256]{1,0:T(8,128)}) %all-reduce.9.cloned.1.call-update) | async-done | bytes 131088 | tf_op jit(solution)/shard_map/psum | solution.py:11
  290.9 2.2 convolution_subtract_fusion
  (42 shorter events, 2.8 us)
Async XLA Ops:
  7.2 76.6 %all-reduce.5.cloned.1.call-start = ((), (), s32[]{:S(2)}) async-start(), calls=%async_computation.1 | async-start | bytes 6291456 | tf_op jit(solution)/shard_map/psum | solution.py:11
  12.5 147.2 %all-reduce.7.cloned.1.call-start = ((), (), s32[]{:S(2)}) async-start(), calls=%async_computation.2 | async-start | bytes 524288 | tf_op jit(solution)/shard_map/psum | solution.py:53
  88.3 137.4 %reduce-scatter.4.cloned.1.call-start = ((), (), s32[]{:S(2)}) async-start(), calls=%async_computation.4 | async-start | bytes 589824
  95.0 195.9 %all-reduce.9.cloned.1.call-start = ((), (), s32[]{:S(2)}) async-start(), calls=%async_computation.3 | async-start | bytes 262144 | tf_op jit(solution)/shard_map/psum | solution.py:11
  183.5 107.4 %copy-start.1 = (f32[512,128]{1,0:T(8,128)S(1)}, f32[512,128]{1,0:T(8,128)}, u32[]{:S(2)}) copy-start(f32[512,128]{1,0:T(8,128)} %param.5) | copy-start | bytes 786436
  227.8 65.3 %copy-start = (f32[64,256]{1,0:T(8,128)}, f32[64,256]{1,0:T(8,128)S(1)}, u32[]{:S(2)}) copy-start(f32[64,256]{1,0:T(8,128)S(1)} %fusion.7) | copy-start | bytes 196612
Sparse Core Ops, SparseCore 0:
  12.6 71.1 all-reduce.4
  88.5 71.1 all-reduce.6
  163.0 62.7 reduce-scatter.3
  260.0 30.7 all-reduce.8
where the time goes:
time: 300 us
  waiting for transfers between devices  169 us (56%)
  other arithmetic  61.2 us (20%)
  blocking collectives  31.4 us (10%)
  between operations  16.7 us (6%)
  matrix products  13.6 us (5%)
  local copies, waits for them, and re-layouts  6.6 us (2%)
    psum x2, waiting for transfers between devices, spread(): return lax.psum(block, axis)  101 us
    psum x1, waiting for transfers between devices, local(): diagonal = lax.psum(own_block, 'col')  64.4 us
    another operation x6, other arithmetic, local(): lower = jnp.linalg.cholesky(diagonal)  34 us
    all_gather x1, blocking collectives, local(): factor_block = lax.all_gather(factor_mine, 'col', axis=0, tiled=True)  31.4 us
    another operation x3, other arithmetic, solve_rows(): return jax.scipy.linalg.solve_triangular(lower, panel_rows.T, lower=True).T  19.7 us
  transfers between devices with their start and end apart: 4, of which 4 were waited for; matrix products, arithmetic and copies ran while one was open for 23% of the time, Pallas kernels for 0%

commit v1 on v0

--- a/solution.py
+++ b/solution.py
@@ -1,9 +1,27 @@
+import functools
 import jax
 import jax.numpy as jnp
 from jax import lax
 from jax.sharding import PartitionSpec as P
 
 PANEL = 256
+
+
+def lift_cards_now(slab_in, ax_name):
+    nodes = lax.axis_size(ax_name)
+    inbox = tuple(((no, (no + 1) % nodes) for no in range(nodes)))
+
+    def change_edge(all_rows):
+        if len(all_rows) == nodes:
+            return all_rows
+        return change_edge([lax.ppermute(all_rows[0], axis_name=ax_name, perm=inbox), *all_rows])
+
+    f_next = change_edge([slab_in])
+    earlier = jnp.concatenate(f_next, axis=0)
+    return jnp.roll(earlier, (lax.axis_index(ax_name) + 1) * slab_in.shape[0], axis=0)
+
+
+rest_wires = functools.partial(lift_cards_now, ax_name="col")
 
 
 def spread(block, axis, owner):
@@ -55,7 +73,7 @@
     lower = jnp.linalg.cholesky(diagonal)
     factor_mine = solve_rows(lower, mine_rows)
     factor_mine = mask_above(factor_mine, row_pos * rows_dev + col_pos * row_share, panel_start)
-    factor_block = lax.all_gather(factor_mine, "col", axis=0, tiled=True)
+    factor_block = rest_wires(factor_mine)
     window_start = panel_start + PANEL + col_pos * tile_cols
     window_owner = window_start // rows_dev
     window_cut = lax.dynamic_slice_in_dim(factor_block, window_start % rows_dev, tile_cols, 0)

time: 300 us -> 316 us (1.053)
  waiting for transfers between devices: 169 us -> 215 us
  blocking collectives: 31.4 us -> 0 us
    ppermute x0 -> x7, waiting for transfers between devices: none -> 47.6 us  [change_edge(): lax.ppermute(all_rows[0], axis_name=ax_name, perm=inbox)]
    all_gather x1 -> x0, blocking collectives: 31.4 us -> none  [local(): factor_block = lax.all_gather(factor_mine, 'col', axis=0, tiled=True)]
  transfers between devices with their start and end apart: 4 -> 11, of which waited for: 4 -> 11; matrix products, arithmetic and copies ran while one was open for 23% -> 21% of each run, Pallas kernels for 0% -> 0%
where the time goes in v1:
time: 316 us; the launch traced here: 315 us
  waiting for transfers between devices  215 us (68%)
  other arithmetic  61.2 us (19%)
  between operations  16.8 us (5%)
  matrix products  13.6 us (4%)
  local copies, waits for them, and re-layouts  6.76 us (2%)
    psum x2, waiting for transfers between devices, spread(): return lax.psum(block, axis)  99.7 us
    psum x1, waiting for transfers between devices, local(): diagonal = lax.psum(own_block, 'col')  64.4 us
    ppermute x7, waiting for transfers between devices, change_edge(): lax.ppermute(all_rows[0], axis_name=ax_name, perm=inbox)  47.6 us
    another operation x6, other arithmetic, local(): lower = jnp.linalg.cholesky(diagonal)  34 us
    another operation x3, other arithmetic, solve_rows(): return jax.scipy.linalg.solve_triangular(lower, panel_rows.T, lower=True).T  19.7 us
  transfers between devices with their start and end apart: 11, of which 11 were waited for; matrix products, arithmetic and copies ran while one was open for 21% of the time, Pallas kernels for 0%

profile of v1, /device:TPU:0, one launch (start us, length us, event | category | flops | bytes accessed | tf_op | source)
XLA Modules:
  0.0 315.2 jit_solution(15775272627234800372)
XLA Ops:
  7.9 4.5 %dynamic-slice_select_fusion = bf16[256,6144]{1,0:T(8,128)(2,1)} fusion(bf16[512,6144]{1,0:T(8,128)(2,1)} %param.4, s32[]{:T(128)S(6)} %select_n.78, pred[]{:T(512)S(6)} %eq.18), kind=kLoop, calls=%fused_computation.2 | loop fusion | flops 1572864 | bytes 6291461 | tf_op jit(solution)/shard_map/jit(_where)/select_n | solution.py:28
  13.2 70.5 %all-reduce.5.cloned.1.call-done = bf16[256,6144]{1,0:T(8,128)(2,1)} async-done(((bf16[256,6144]{1,0:T(8,128)(2,1)}), bf16[256,6144]{1,0:T(8,128)(2,1)}) %all-reduce.5.cloned.1.call-update) | async-done | bytes 3145744 | tf_op jit(solution)/shard_map/psum | solution.py:29
  83.7 4.6 %fusion.12 = f32[256,256]{0,1:T(8,128)} fusion(bf16[256,6144]{1,0:T(8,128)(2,1)} %all-reduce.5.cloned.1.call-done), kind=kOutput, calls=%fused_computation.57 | convolution fusion | flops 805306368 | bytes 3407872 | tf_op jit(solution)/shard_map/dot_general | solution.py:68
  88.4 5.6 %convolution_bitcast_fusion = f32[512,256]{0,1:T(8,128)S(1)} fusion(bf16[256,6144]{1,0:T(8,128)(2,1)} %all-reduce.5.cloned.1.call-done, bf16[512,6144]{1,0:T(8,128)(2,1)} %param.4), kind=kOutput, calls=%fused_computation.3 | convolution fusion | flops 1610612736 | bytes 9961472 | tf_op jit(solution)/shard_map/dot_general | solution.py:60
  95.2 64.4 %all-reduce.7.cloned.1.call-done = f32[256,256]{0,1:T(8,128)} async-done(((f32[256,256]{0,1:T(8,128)}), f32[256,256]{0,1:T(8,128)}) %all-reduce.7.cloned.1.call-update) | async-done | bytes 262160 | tf_op jit(solution)/shard_map/psum | solution.py:71
  160.8 1.1 fusion.1
  161.9 11.7 %cholesky.49 = f32[128,128]{1,0:T(8,128)S(1)} custom-call(f32[128,128]{1,0:T(8,128)S(1)} %cholesky.115), custom_call_target="Cholesky" | custom-call | tf_op jit(solution)/shard_map/jit(cholesky)/cholesky | solution.py:73
  173.6 9.8 %custom-call.15 = f32[1,128,128]{1,2,0:T(8,128)S(1)} custom-call(f32[1,128,128]{2,1,0:T(8,128)S(1)} %get-tuple-element.29), custom_call_target="InvertDiagBlocksLowerTriangular" | custom-call | tf_op jit(solution)/shard_map/jit(cholesky)/cholesky | solution.py:73
  183.9 11.7 %cholesky.103 = f32[128,128]{1,0:T(8,128)S(1)} custom-call(f32[128,128]{1,0:T(8,128)S(1)} %convolution_subtract_fusion.2), custom_call_target="Cholesky" | custom-call | tf_op jit(solution)/shard_map/jit(cholesky)/cholesky | solution.py:73
  198.2 4.5 %while.1 = (s32[]{:T(128)}, f32[256,256]{0,1:T(8,128)S(1)}, s32[2,2]{1,0:T(2,128)S(1)}, f32[2,128,128]{2,1,0:T(8,128)S(1)}, s32[]{:T(128)}) while((s32[]{:T(128)}, f32[256,256]{0,1:T(8,128)S(1)}, s32[2,2]{1,0:T(2,128)S(1)}, f32[2,128,128]{2,1,0:T(8,128)S(1)}, s32[]{:T(128)}) %tuple.27), condition=%wide.while_cond, body=%wide.while_body.sunk | while | flops 2 | bytes 393321 | solution.py:44
  199.0 1.4 dynamic-slice.7
  201.1 1.4 dynamic-slice.7
  202.7 19.7 %custom-call.16 = f32[2,128,128]{1,2,0:T(8,128)S(1)} custom-call(f32[2,128,128]{2,1,0:T(8,128)S(1)} %get-tuple-element.9), custom_call_target="InvertDiagBlocksLowerTriangular" | custom-call | tf_op jit(solution)/shard_map/jit(_solve_triangular)/triangular_solve | solution.py:44
  222.4 3.0 reduce-scatter.4.cloned.1.call-done
  227.4 1.4 collective-permute-start
  228.8 5.6 %collective-permute-done = f32[64,256]{1,0:T(8,128)S(1)} collective-permute-done((f32[64,256]{1,0:T(8,128)S(1)}, f32[64,256]{1,0:T(8,128)S(1)}, u32[]{:S(2)}, u32[]{:S(2)}) %collective-permute-start) | collective-permute-done | bytes 65568 | tf_op jit(solution)/shard_map/ppermute | solution.py:17
  234.4 7.0 %collective-permute-done.1 = f32[64,256]{1,0:T(8,128)S(1)} collective-permute-done((f32[64,256]{1,0:T(8,128)S(1)}, f32[64,256]{1,0:T(8,128)S(1)}, u32[]{:S(2)}, u32[]{:S(2)}) %collective-permute-start.1) | collective-permute-done | bytes 65568 | tf_op jit(solution)/shard_map/ppermute | solution.py:17
  241.4 7.2 %collective-permute-done.2 = f32[64,256]{1,0:T(8,128)S(1)} collective-permute-done((f32[64,256]{1,0:T(8,128)S(1)}, f32[64,256]{1,0:T(8,128)S(1)}, u32[]{:S(2)}, u32[]{:S(2)}) %collective-permute-start.2) | collective-permute-done | bytes 65568 | tf_op jit(solution)/shard_map/ppermute | solution.py:17
  248.6 7.0 %collective-permute-done.3 = f32[64,256]{1,0:T(8,128)S(1)} collective-permute-done((f32[64,256]{1,0:T(8,128)S(1)}, f32[64,256]{1,0:T(8,128)S(1)}, u32[]{:S(2)}, u32[]{:S(2)}) %collective-permute-start.3) | collective-permute-done | bytes 65568 | tf_op jit(solution)/shard_map/ppermute | solution.py:17
  255.5 7.0 %collective-permute-done.4 = f32[64,256]{1,0:T(8,128)S(1)} collective-permute-done((f32[64,256]{1,0:T(8,128)S(1)}, f32[64,256]{1,0:T(8,128)S(1)}, u32[]{:S(2)}, u32[]{:S(2)}) %collective-permute-start.4) | collective-permute-done | bytes 65568 | tf_op jit(solution)/shard_map/ppermute | solution.py:17
  262.5 7.0 %collective-permute-done.5 = f32[64,256]{1,0:T(8,128)S(1)} collective-permute-done((f32[64,256]{1,0:T(8,128)S(1)}, f32[64,256]{1,0:T(8,128)S(1)}, u32[]{:S(2)}, u32[]{:S(2)}) %collective-permute-start.5) | collective-permute-done | bytes 65568 | tf_op jit(solution)/shard_map/ppermute | solution.py:17
  269.5 7.0 %collective-permute-done.6 = f32[64,256]{1,0:T(8,128)S(1)} collective-permute-done((f32[64,256]{1,0:T(8,128)S(1)}, f32[64,256]{1,0:T(8,128)S(1)}, u32[]{:S(2)}, u32[]{:S(2)}) %collective-permute-start.6) | collective-permute-done | bytes 65568 | tf_op jit(solution)/shard_map/ppermute | solution.py:17
  277.3 29.2 %all-reduce.9.cloned.1.call-done = f32[128,256]{1,0:T(8,128)} async-done(((f32[128,256]{1,0:T(8,128)}), f32[128,256]{1,0:T(8,128)}) %all-reduce.9.cloned.1.call-update) | async-done | bytes 131088 | tf_op jit(solution)/shard_map/psum | solution.py:29
  306.5 2.2 convolution_subtract_fusion
  (71 shorter events, 8.4 us)
Async XLA Ops:
  7.2 76.6 %all-reduce.5.cloned.1.call-start = ((), (), s32[]{:S(2)}) async-start(), calls=%async_computation.1 | async-start | bytes 6291456 | tf_op jit(solution)/shard_map/psum | solution.py:29
  12.4 147.2 %all-reduce.7.cloned.1.call-start = ((), (), s32[]{:S(2)}) async-start(), calls=%async_computation.2 | async-start | bytes 524288 | tf_op jit(solution)/shard_map/psum | solution.py:71
  88.3 137.1 %reduce-scatter.4.cloned.1.call-start = ((), (), s32[]{:S(2)}) async-start(), calls=%async_computation.4 | async-start | bytes 589824
  95.0 211.6 %all-reduce.9.cloned.1.call-start = ((), (), s32[]{:S(2)}) async-start(), calls=%async_computation.3 | async-start | bytes 262144 | tf_op jit(solution)/shard_map/psum | solution.py:29
  198.1 108.4 %copy-start.1 = (f32[512,128]{1,0:T(8,128)S(1)}, f32[512,128]{1,0:T(8,128)}, u32[]{:S(2)}) copy-start(f32[512,128]{1,0:T(8,128)} %param.5) | copy-start | bytes 786436
  227.4 81.3 %copy-start = (f32[64,256]{1,0:T(8,128)}, f32[64,256]{1,0:T(8,128)S(1)}, u32[]{:S(2)}) copy-start(f32[64,256]{1,0:T(8,128)S(1)} %fusion.8) | copy-start | bytes 196612
  227.4 7.0 %collective-permute-start = (f32[64,256]{1,0:T(8,128)S(1)}, f32[64,256]{1,0:T(8,128)S(1)}, u32[]{:S(2)}, u32[]{:S(2)}) collective-permute-start(f32[64,256]{1,0:T(8,128)S(1)} %fusion.8), channel_id=1, source_target_pairs={{0,1},{1,2},{2,3},{3,4},{4,5},{5,6},{6,7},{7,0},{8,9},{9,10},{10,1... | collective-permute-start | bytes 196616 | tf_op jit(solution)/shard_map/ppermute | solution.py:17
  234.4 7.0 %collective-permute-start.1 = (f32[64,256]{1,0:T(8,128)S(1)}, f32[64,256]{1,0:T(8,128)S(1)}, u32[]{:S(2)}, u32[]{:S(2)}) collective-permute-start(f32[64,256]{1,0:T(8,128)S(1)} %collective-permute-done), channel_id=1, source_target_pairs={{0,1},{1,2},{2,3},{3,4},{4,5},{5,6},{6,7},{7,0},{8,9},{9,10},{10,1... | collective-permute-start | bytes 196616 | tf_op jit(solution)/shard_map/ppermute | solution.py:17
  241.4 7.2 %collective-permute-start.2 = (f32[64,256]{1,0:T(8,128)S(1)}, f32[64,256]{1,0:T(8,128)S(1)}, u32[]{:S(2)}, u32[]{:S(2)}) collective-permute-start(f32[64,256]{1,0:T(8,128)S(1)} %collective-permute-done.1), channel_id=1, source_target_pairs={{0,1},{1,2},{2,3},{3,4},{4,5},{5,6},{6,7},{7,0},{8,9},{9,10},{10,1... | collective-permute-start | bytes 196616 | tf_op jit(solution)/shard_map/ppermute | solution.py:17
  248.6 7.0 %collective-permute-start.3 = (f32[64,256]{1,0:T(8,128)S(1)}, f32[64,256]{1,0:T(8,128)S(1)}, u32[]{:S(2)}, u32[]{:S(2)}) collective-permute-start(f32[64,256]{1,0:T(8,128)S(1)} %collective-permute-done.2), channel_id=1, source_target_pairs={{0,1},{1,2},{2,3},{3,4},{4,5},{5,6},{6,7},{7,0},{8,9},{9,10},{10,1... | collective-permute-start | bytes 196616 | tf_op jit(solution)/shard_map/ppermute | solution.py:17
  255.5 7.0 %collective-permute-start.4 = (f32[64,256]{1,0:T(8,128)S(1)}, f32[64,256]{1,0:T(8,128)S(1)}, u32[]{:S(2)}, u32[]{:S(2)}) collective-permute-start(f32[64,256]{1,0:T(8,128)S(1)} %collective-permute-done.3), channel_id=1, source_target_pairs={{0,1},{1,2},{2,3},{3,4},{4,5},{5,6},{6,7},{7,0},{8,9},{9,10},{10,1... | collective-permute-start | bytes 196616 | tf_op jit(solution)/shard_map/ppermute | solution.py:17
  262.5 7.0 %collective-permute-start.5 = (f32[64,256]{1,0:T(8,128)S(1)}, f32[64,256]{1,0:T(8,128)S(1)}, u32[]{:S(2)}, u32[]{:S(2)}) collective-permute-start(f32[64,256]{1,0:T(8,128)S(1)} %collective-permute-done.4), channel_id=1, source_target_pairs={{0,1},{1,2},{2,3},{3,4},{4,5},{5,6},{6,7},{7,0},{8,9},{9,10},{10,1... | collective-permute-start | bytes 196616 | tf_op jit(solution)/shard_map/ppermute | solution.py:17
  269.5 7.0 %collective-permute-start.6 = (f32[64,256]{1,0:T(8,128)S(1)}, f32[64,256]{1,0:T(8,128)S(1)}, u32[]{:S(2)}, u32[]{:S(2)}) collective-permute-start(f32[64,256]{1,0:T(8,128)S(1)} %collective-permute-done.5), channel_id=1, source_target_pairs={{0,1},{1,2},{2,3},{3,4},{4,5},{5,6},{6,7},{7,0},{8,9},{9,10},{10,1... | collective-permute-start | bytes 196616 | tf_op jit(solution)/shard_map/ppermute | solution.py:17
Sparse Core Ops, SparseCore 0:
  12.6 71.1 all-reduce.4
  88.4 71.1 all-reduce.6
  162.9 62.3 reduce-scatter.3
  277.5 28.9 all-reduce.8
